TPU v7x, 128 devices: a whole 4x4x4 slice. The times are simulated.
128 devices in a mesh: aux: 64 (over z, y, x), bas: 2 (over core).
Axes of the slice: x: 4, y: 4, z: 4, core: 2. Of those that a mesh axis runs over, the one named last changes fastest.
Arguments:
- integrals: bfloat16 [64, 128, 3, 128, 128], P('aux', 'bas'), may hold values from -0.0625 to 0.0625
- orbitals: bfloat16 [128, 128, 128], P('bas'), may hold values from -0.5 to 0.5
- locality: int32 [128], P('bas'), may hold values from 0 to 63, as said below
- screen: int32 [64, 128, 3], P('aux', 'bas'), may hold values 0 or 1
- metric: bfloat16 [64, 64], replicated, may hold values from -1 to 3
Outputs:
- exchange_band: float32 [128, 5, 16384], P('bas', None, 'aux')
Inputs may be any that keep to these rules, and one draw needn't show every extreme that they name: `locality`: within each bas shard, its 64 orbital tiles name each of its 64 blocks exactly once.
All inputs are finite; a program needn't handle non-finite values. No bound on the sum of `screen` on one device may be relied on, other than what follows from the above.
Results may differ from a plain program's by a relative error of at most 0.00096.
Values may be sent and summed in bfloat16 or wider, within the bound.
A program may use at most 128 MiB of HBM per device.

v0:
```python
import jax
import jax.numpy as jnp
from jax import lax
from jax.sharding import PartitionSpec as P


def passed_along(value, axis, steps):
    count = lax.axis_size(axis)
    first, last = (max(0, -steps), min(count, count - steps))
    return lax.ppermute(value, axis, [(source, source + steps) for source in range(first, last)])


def metric_apply(metric, exchanged):
    slab_rows = exchanged[0]
    product = jnp.dot(
        metric, slab_rows.reshape(slab_rows.shape[0], -1), preferred_element_type=jnp.float32
    )
    results = [product.astype(jnp.bfloat16).reshape(slab_rows.shape)]
    return jnp.stack(results)


def add_band(window, gram_block, row_first):
    reach_width = gram_block.shape[0]
    for offset in range(reach_width):
        band_piece = jnp.transpose(gram_block[offset], (1, 0, 2))
        band_piece = jnp.pad(band_piece, ((reach_width - 1 - offset, offset), (0, 0), (0, 0)))
        start_row = row_first + offset
        current = lax.dynamic_slice_in_dim(window, start_row, 1, 0)
        window = lax.dynamic_update_slice_in_dim(window, current + band_piece[None], start_row, 0)
    return window


def body(integrals, orbitals, locality, screen, metric):
    aux_rows, block_count, reach_width, tile_size, _ = integrals.shape
    reach_blocks = reach_width // 2
    orbital_count = orbitals.shape[0]
    per_device = orbital_count // lax.axis_size("aux")
    first_block = lax.axis_index("bas") * block_count
    total_blocks = block_count * lax.axis_size("bas")
    chosen = jnp.take(integrals, locality, axis=1)
    half_rows = lax.dot_general(
        chosen, orbitals, (((4,), (1,)), ((1,), (0,))), preferred_element_type=jnp.float32
    )
    offsets = jnp.arange(reach_width, dtype=jnp.int32)
    row_blocks = first_block + locality[:, None] + offsets[None, :] - reach_blocks
    inside = ((row_blocks >= 0) & (row_blocks < total_blocks)).astype(jnp.float32)
    keep_mask = screen[0].astype(jnp.float32) * inside
    half_rows = (half_rows * keep_mask[:, None, :, None, None]).astype(jnp.bfloat16)
    mixed_rows = metric_apply(
        metric, lax.all_to_all(half_rows, "aux", split_axis=0, concat_axis=1, tiled=True)
    )
    mine = lax.dynamic_slice_in_dim(locality, lax.axis_index("aux") * per_device, per_device, 0)
    window = jnp.zeros(
        (block_count + 2 * reach_blocks, 2 * reach_width - 1, tile_size, tile_size), jnp.float32
    )
    fitted = mixed_rows[0]
    gram_block = lax.dot_general(
        fitted, fitted, (((0, 3), (0, 3)), ((), ())), preferred_element_type=jnp.float32
    )
    window = add_band(window, gram_block, mine[0])
    lower_rim = window[:reach_blocks]
    upper_rim = window[reach_blocks + block_count :]
    own_rows = window[reach_blocks : reach_blocks + block_count]
    from_below = passed_along(upper_rim.astype(jnp.bfloat16), "bas", 1).astype(upper_rim.dtype)
    from_above = passed_along(lower_rim.astype(jnp.bfloat16), "bas", -1).astype(lower_rim.dtype)
    own_rows = own_rows.at[:reach_blocks].add(from_below)
    own_rows = own_rows.at[block_count - reach_blocks :].add(from_above)
    flat_rows = own_rows.reshape(block_count, 2 * reach_width - 1, tile_size * tile_size)
    return lax.psum_scatter(flat_rows, "aux", scatter_dimension=2, tiled=True)


def solution(mesh):
    placed = (
        P("aux", "bas", None, None, None),
        P("bas", None, None),
        P("bas"),
        P("aux", "bas", None),
        P(),
    )
    return jax.shard_map(
        body, mesh=mesh, in_specs=placed, out_specs=P("bas", None, "aux"), check_vma=False
    )
```

profile of v0, /device:TPU:0, one launch (start us, length us, event | category | flops | bytes accessed | tf_op | source)
XLA Modules:
  0.0 615.4 jit_solution(4274369219538918507)
XLA Ops:
  6.5 0.0 copy-start
  6.5 0.8 compare_and_fusion
  7.3 0.7 compare_select_fusion
  8.0 0.7 convert_element_type.37
  8.7 0.1 copy.14
  8.8 6.8 %gather_fusion = bf16[64,3,128,128]{3,2,1,0:T(8,128)(2,1)} fusion(bf16[64,3,128,128]{3,2,1,0:T(8,128)(2,1)} %bitcast.62, s32[1024]{0:T(1024)S(1)} %pad_clamp_fusion), kind=kCustom, calls=%fused_computation | custom fusion | bytes 12583168 | tf_op jit(solution)/shard_map/jit(_take)/gather | solution.py:40
  15.6 0.0 copy-done
  15.6 7.3 %fusion = bf16[64,1,3,128,128]{4,3,2,1,0:T(8,128)(2,1)} fusion(f32[64,3]{1,0:T(8,128)S(1)} %copy.14, bf16[64,3,128,128]{3,2,1,0:T(8,128)(2,1)} %gather_fusion, pred[64]{0:T(512)(128)(4,1)S(1)} %compare_and_fusion, bf16[64,128,128]{2,1,0:T(8,128)(2,1)S(1)} %copy-done), kind=kOutput, calls=%fused_computation.3 | convolution fusion | flops 814743552 | bytes 14680896 | tf_op jit(solution)/shard_map/dot_general | solution.py:41
  22.9 11.9 %all-to-all-start = ((bf16[64,1,3,128,128]{4,3,2,1,0:T(8,128)(2,1)}), bf16[64,1,3,128,128]{4,3,2,1,0:T(8,128)(2,1)}, u32[]{:S(2)}, u32[]{:S(2)}) async-start(bf16[64,1,3,128,128]{4,3,2,1,0:T(8,128)(2,1)} %fusion), calls=%async_computation | async-start | bytes 12582912 | tf_op jit(solution)/shard_map/all_to_all | solution.py:50
  34.7 0.2 reduce-scatter.2.cloned.1.call-start
  35.0 0.6 dynamic_slice.9
  40.1 75.4 %all-to-all-done = bf16[64,1,3,128,128]{4,3,2,1,0:T(8,128)(2,1)} async-done(((bf16[64,1,3,128,128]{4,3,2,1,0:T(8,128)(2,1)}), bf16[64,1,3,128,128]{4,3,2,1,0:T(8,128)(2,1)}, u32[]{:S(2)}, u32[]{:S(2)}) %all-to-all-start) | async-done | bytes 6291488 | tf_op jit(solution)/shard_map/all_to_all | solution.py:50
  115.5 7.7 %fusion.13 = bf16[8,8,384,128]{3,1,2,0:T(8,128)(2,1)S(1)} fusion(bf16[64,64]{1,0:T(8,128)(2,1)S(1)} %copy-done.3, bf16[8,8,384,128]{3,2,1,0:T(8,128)(2,1)} %bitcast.27), kind=kOutput, calls=%fused_computation.14 | convolution fusion | flops 405798912 | bytes 12591104 | tf_op jit(solution)/shard_map/dot_general | solution.py:15
  123.1 1.7 copy.26
  124.9 3.4 fusion.17
  128.4 9.9 %broadcast_in_dim.27 = f32[66,5,128,128]{3,2,1,0:T(8,128)} broadcast(f32[]{:T(128)} %constant.85.clone.1), dimensions={} | broadcast | bytes 21626884 | tf_op jit(solution)/shard_map/broadcast_in_dim | solution.py:53
  138.3 0.8 bitcast_dynamic-update-slice_fusion
  139.1 1.7 fusion.25
  140.8 1.7 fusion.24
  142.5 8.6 %convert.4 = bf16[66,5,128,128]{3,2,1,0:T(8,128)(2,1)S(1)} convert(f32[66,5,128,128]{3,2,1,0:T(8,128)} %fusion.24) | non-fusion elementwise | flops 5406720 | bytes 32440320 | tf_op jit(solution)/shard_map/convert.1
  151.1 1.6 collective-permute-start
  152.7 3.2 copy-done.2
  155.9 7.4 %slice.92 = f32[64,5,128,128]{3,2,1,0:T(8,128)} slice(f32[66,5,128,128]{3,2,1,0:T(8,128)S(1)} %copy-done.2), slice={[1:65], [0:5], [0:128], [0:128]} | slice | bytes 41943040 | tf_op jit(solution)/shard_map/slice | solution.py:63
  163.3 1.3 collective-permute-start.1
  164.6 0.0 collective-permute-done
  164.6 0.8 fusion.23
  165.4 1.2 collective-permute-done.1
  166.6 1.7 fusion.22
  168.3 16.1 %copy.18 = f32[64,5,128,128]{3,2,0,1:T(8,128)} copy(f32[64,5,128,128]{3,2,1,0:T(8,128)} %fusion.22) | data formatting | bytes 41943040 | tf_op jit(solution)/shard_map/scatter-add | solution.py:67
  184.4 22.7 %reshape.123 = f32[64,5,16384]{2,0,1:T(8,128)} reshape(f32[64,5,128,128]{3,2,0,1:T(8,128)} %copy.18) | data formatting | bytes 41943040 | tf_op jit(solution)/shard_map/reshape | solution.py:68
  207.1 0.0 reduce-scatter.2.cloned.1.call-update
  207.1 401.4 %reduce-scatter.2.cloned.1.call-done = f32[64,5,256]{2,0,1:T(8,128)} async-done(((f32[64,5,16384]{2,0,1:T(8,128)}), f32[64,5,256]{2,0,1:T(8,128)}) %reduce-scatter.2.cloned.1.call-update) | async-done | bytes 327696 | tf_op jit(solution)/shard_map/reduce_scatter | solution.py:69
  (11 shorter events, 0.1 us)
Async XLA Ops:
  6.5 9.0 %copy-start = (bf16[64,128,128]{2,1,0:T(8,128)(2,1)S(1)}, bf16[64,128,128]{2,1,0:T(8,128)(2,1)}, u32[]{:S(2)}) copy-start(bf16[64,128,128]{2,1,0:T(8,128)(2,1)} %param.10) | copy-start | bytes 6291460
  22.9 12.1 %copy-start.4 = (s32[64]{0:T(128)S(1)}, s32[64]{0:T(128)}, u32[]{:S(2)}) copy-start(s32[64]{0:T(128)} %param.11) | copy-start | bytes 772
  22.9 92.6 %copy-start.3 = (bf16[64,64]{1,0:T(8,128)(2,1)S(1)}, bf16[64,64]{1,0:T(8,128)(2,1)}, u32[]{:S(2)}) copy-start(bf16[64,64]{1,0:T(8,128)(2,1)} %param.13) | copy-start | bytes 24580
  22.9 92.6 %all-to-all-start = ((bf16[64,1,3,128,128]{4,3,2,1,0:T(8,128)(2,1)}), bf16[64,1,3,128,128]{4,3,2,1,0:T(8,128)(2,1)}, u32[]{:S(2)}, u32[]{:S(2)}) async-start(bf16[64,1,3,128,128]{4,3,2,1,0:T(8,128)(2,1)} %fusion), calls=%async_computation | async-start | bytes 12582912 | tf_op jit(solution)/shard_map/all_to_all | solution.py:50
  34.7 573.8 %reduce-scatter.2.cloned.1.call-start = ((), (), s32[]{:S(2)}) async-start(), calls=%async_computation.2 | async-start | bytes 21299200 | tf_op jit(solution)/shard_map/reduce_scatter | solution.py:69
  142.5 13.4 %copy-start.2 = (f32[66,5,128,128]{3,2,1,0:T(8,128)S(1)}, f32[66,5,128,128]{3,2,1,0:T(8,128)}, u32[]{:S(2)}) copy-start(f32[66,5,128,128]{3,2,1,0:T(8,128)} %fusion.24) | copy-start | bytes 64880644
  151.1 13.5 %collective-permute-start = (bf16[1,5,128,128]{3,2,1,0:T(8,128)(2,1)S(1)}, bf16[1,5,128,128]{3,2,1,0:T(8,128)(2,1)S(1)}, u32[]{:S(2)}, u32[]{:S(2)}) collective-permute-start(bf16[1,5,128,128]{3,2,1,0:T(8,128)(2,1)S(1)} %get-tuple-element.30), channel_id=1, source_target_pairs={{0,1},{2,3},{4,5},{6,7},{8,9},{10,11},{12,13},{14,15},{16,17},{18,... | collective-permute-start | bytes 491528 | tf_op jit(solution)/shard_map/ppermute | solution.py:10
  163.3 3.3 collective-permute-start.1
  207.1 401.5 %copy-start.1 = (bf16[64,128,128]{2,1,0:T(8,128)(2,1)S(1)}, bf16[64,128,128]{2,1,0:T(8,128)(2,1)}, u32[]{:S(2)}) copy-start(bf16[64,128,128]{2,1,0:T(8,128)(2,1)} %param.10) | copy-start | bytes 6291460
Sparse Core Ops, SparseCore 0:
  207.2 401.2 reduce-scatter.1
where the time goes:
time: 616 us; the launch traced here: 615 us
  waiting for transfers between devices  478 us (78%)
  local copies, waits for them, and re-layouts  69.3 us (11%)
  matrix products  18.4 us (3%)
  between operations  18 us (3%)
  other arithmetic  16.7 us (3%)
  starting transfers between devices  14.9 us (2%)
    reduce_scatter x1, waiting for transfers between devices, body(): return lax.psum_scatter(flat_rows, 'aux', scatter_dimension=2, tiled=True)  401 us
    all_to_all x1, waiting for transfers between devices, body(): lax.all_to_all(half_rows, 'aux', split_axis=0, concat_axis=1, tiled=True)  75.4 us
    reshape x1, local copies, waits for them, and re-layouts, body(): own_rows.reshape(block_count, 2 * reach_width - 1, tile_size * tile_size)  22.7 us
    scatter-add x1, local copies, waits for them, and re-layouts, body(): own_rows = own_rows.at[block_count - reach_blocks:].add(from_above)  16.1 us
  transfers between devices with their start and end apart: 4, of which 3 were waited for; matrix products, arithmetic and copies ran while one was open for 1% of the time, Pallas kernels for 0%

commit v1 on v0

v1 whole, which is shorter than its diff:
```python
import jax
import jax.numpy as jnp
from jax import lax
from jax.sharding import PartitionSpec as P


def metric_apply(metric, slab_rows):
    product = jnp.dot(
        metric, slab_rows.reshape(slab_rows.shape[0], -1), preferred_element_type=jnp.float32
    )
    return product.astype(jnp.bfloat16).reshape(slab_rows.shape)


def body(integrals, orbitals, locality, screen, metric):
    aux_rows, block_count, reach, tile, _ = integrals.shape
    n_aux = lax.axis_size("aux")
    first_block = lax.axis_index("bas") * block_count
    total_blocks = block_count * lax.axis_size("bas")
    chosen = jnp.take(integrals, locality, axis=1)
    half_rows = lax.dot_general(
        chosen, orbitals, (((4,), (1,)), ((1,), (0,))), preferred_element_type=jnp.float32
    )
    offsets = jnp.arange(reach, dtype=jnp.int32)
    row_blocks = first_block + locality[:, None] + offsets[None, :] - 1
    inside = ((row_blocks >= 0) & (row_blocks < total_blocks)).astype(jnp.float32)
    keep_mask = screen[0].astype(jnp.float32) * inside
    half_rows = (half_rows * keep_mask[:, None, :, None, None]).astype(jnp.bfloat16)
    received = lax.all_to_all(half_rows, "aux", split_axis=0, concat_axis=1, tiled=True)
    fitted = metric_apply(metric, received[0])
    gram = lax.dot_general(
        fitted, fitted, (((0, 3), (0, 3)), ((), ())), preferred_element_type=jnp.float32
    )
    share = tile * tile // n_aux
    pieces = jnp.transpose(gram, (0, 2, 1, 3)).reshape(reach * reach, n_aux, share)
    pieces = jnp.transpose(pieces, (1, 0, 2))
    shares = lax.all_to_all(pieces, "aux", split_axis=0, concat_axis=0, tiled=True)
    ids = jnp.arange(block_count, dtype=jnp.int32)
    order = jnp.sum(jnp.where(locality[None, :] == ids[:, None], ids[None, :], 0), axis=1)
    by_block = jnp.take(shares, order, axis=0).reshape(block_count, reach, reach, share)
    padded = [
        jnp.pad(by_block[:, d], ((0, 0), (reach - 1 - d, d), (0, 0))) for d in range(reach)
    ]
    zero_row = jnp.zeros((1,) + padded[0].shape[1:], jnp.float32)
    from_below = lax.ppermute(padded[2][-1:], "bas", [(0, 1)])
    from_above = lax.ppermute(padded[0][:1], "bas", [(1, 0)])
    lower = jnp.concatenate([padded[0][1:], from_above], axis=0)
    upper = jnp.concatenate([from_below, padded[2][:-1]], axis=0)
    return lower + padded[1] + upper


def solution(mesh):
    placed = (
        P("aux", "bas", None, None, None),
        P("bas", None, None),
        P("bas"),
        P("aux", "bas", None),
        P(),
    )
    return jax.shard_map(
        body, mesh=mesh, in_specs=placed, out_specs=P("bas", None, "aux"), check_vma=False
    )
```

time: 616 us -> 148 us (0.24)
  waiting for transfers between devices: 478 us -> 19.7 us
  blocking collectives: 0 us -> 86.3 us
  local copies, waits for them, and re-layouts: 69.3 us -> 13.4 us
  between operations: 18 us -> 0.16 us
  other arithmetic: 16.7 us -> 3.2 us
    reduce_scatter x1 -> x0, waiting for transfers between devices: 401 us -> none  [body(): return lax.psum_scatter(flat_rows, 'aux', scatter_dimension=2, tiled=True)]
    all_to_all x0 -> x1, blocking collectives: none -> 86.3 us  [body(): lax.all_to_all(half_rows, 'aux', split_axis=0, concat_axis=1, tiled=True)]
    all_to_all x1, waiting for transfers between devices: 75.4 us -> 18.9 us  [body(): lax.all_to_all(pieces, 'aux', split_axis=0, concat_axis=0, tiled=True)]
    reshape x1 -> x2, local copies, waits for them, and re-layouts: 22.7 us -> 1.5 us  [body(): jnp.transpose(gram, (0, 2, 1, 3)).reshape(reach * reach, n_aux, share)]
    scatter-add x1 -> x0, local copies, waits for them, and re-layouts: 16.1 us -> none  [body(): own_rows = own_rows.at[block_count - reach_blocks:].add(from_above)]
    broadcast_in_dim x1 -> x0, local copies, waits for them, and re-layouts: 9.92 us -> none  [body(): jnp.zeros((block_count + 2 * reach_blocks, 2 * reach_width - 1, tile_size...]
    another operation x1 -> x0, other arithmetic: 8.57 us -> none
    slice x2 -> x3, local copies, waits for them, and re-layouts: 7.42 us -> 0.06 us  [the longest x1 0.05 us: body(): upper = jnp.concatenate([from_below, padded[2][:-1]], axis=0)]
  transfers between devices with their start and end apart: 4 -> 3, of which waited for: 3 -> 2; matrix products, arithmetic and copies ran while one was open for 1% -> 0% of each run, Pallas kernels for 0% -> 0%
where the time goes in v1:
time: 148 us; the launch traced here: 146 us
  blocking collectives  86.3 us (58%)
  waiting for transfers between devices  19.7 us (13%)
  local copies, waits for them, and re-layouts  13.4 us (9%)
  matrix products  12.9 us (9%)
  starting transfers between devices  10.4 us (7%)
  other arithmetic  3.2 us (2%)
    all_to_all x1, blocking collectives, body(): lax.all_to_all(half_rows, 'aux', split_axis=0, concat_axis=1, tiled=True)  86.3 us
    all_to_all x1, waiting for transfers between devices, body(): lax.all_to_all(pieces, 'aux', split_axis=0, concat_axis=0, tiled=True)  18.9 us
    gather x1, local copies, waits for them, and re-layouts, body(): chosen = jnp.take(integrals, locality, axis=1)  6.79 us
    all_to_all x1, starting transfers between devices, body(): lax.all_to_all(pieces, 'aux', split_axis=0, concat_axis=0, tiled=True)  6.04 us
    dot_general x1, matrix products, metric_apply(): jnp.dot(metric, slab_rows.reshape(slab_rows.shape[0], -1), preferred_elem...  4.89 us
    dot_general x1, matrix products, body(): lax.dot_general(chosen, orbitals, (((4,), (1,)), ((1,), (0,))), preferred...  4.63 us
    dot_general x1, matrix products, body(): lax.dot_general(fitted, fitted, (((0, 3), (0, 3)), ((), ())), preferred_e...  3.41 us
    gather x2, local copies, waits for them, and re-layouts, body(): jnp.take(shares, order, axis=0).reshape(block_count, reach, reach, share)  3.17 us
  transfers between devices with their start and end apart: 3, of which 2 were waited for; matrix products, arithmetic and copies ran while one was open for 0% of the time, Pallas kernels for 0%

profile of v1, /device:TPU:0, one launch (start us, length us, event | category | flops | bytes accessed | tf_op | source)
XLA Modules:
  0.0 146.0 jit_solution(4541273412916622637)
XLA Ops:
  0.0 0.0 copy-start
  0.0 0.8 compare_and_fusion
  0.8 0.7 compare_select_fusion.1
  1.5 0.7 convert_element_type.29
  2.2 0.1 copy.25
  2.3 6.8 %gather_fusion = bf16[64,3,128,128]{3,2,1,0:T(8,128)(2,1)} fusion(bf16[64,3,128,128]{3,2,1,0:T(8,128)(2,1)} %bitcast.54, s32[1024]{0:T(1024)S(1)} %pad_clamp_fusion.1), kind=kCustom, calls=%fused_computation | custom fusion | bytes 12583168 | tf_op jit(solution)/shard_map/jit(_take)/gather | solution.py:19
  9.1 0.0 copy-done
  9.1 4.6 %fusion = bf16[64,1,3,128,128]{4,3,2,1,0:T(8,128)(2,1)S(1)} fusion(f32[64,3]{1,0:T(8,128)S(1)} %copy.25, bf16[64,3,128,128]{3,2,1,0:T(8,128)(2,1)} %gather_fusion, pred[64]{0:T(512)(128)(4,1)S(1)} %compare_and_fusion, bf16[64,128,128]{2,1,0:T(8,128)(2,1)S(1)} %copy-done), kind=kOutput, calls=%fused_computation.4 | convolution fusion | flops 814743552 | bytes 14680896 | tf_op jit(solution)/shard_map/dot_general | solution.py:20
  13.7 0.0 copy-start.1
  13.7 86.3 %all_to_all.14 = bf16[64,1,3,128,128]{4,3,2,1,0:T(8,128)(2,1)S(1)} all-to-all(bf16[64,1,3,128,128]{4,3,2,1,0:T(8,128)(2,1)S(1)} %fusion), channel_id=1, replica_groups=mesh['aux'=64,'bas'=2] {'aux'}, dimensions={0} | all-to-all | bytes 12582912 | tf_op jit(solution)/shard_map/all_to_all | solution.py:28
  100.0 0.0 copy-done.1
  100.0 4.9 %fusion.13 = bf16[8,8,384,128]{3,1,2,0:T(8,128)(2,1)S(1)} fusion(bf16[64,64]{1,0:T(8,128)(2,1)S(1)} %copy-done.1, bf16[8,8,384,128]{3,2,1,0:T(8,128)(2,1)S(1)} %bitcast.53), kind=kOutput, calls=%fused_computation.15 | convolution fusion | flops 405798912 | bytes 12591104 | tf_op jit(solution)/shard_map/dot_general | solution.py:8
  104.9 1.7 %copy.38 = bf16[8,8,384,128]{3,2,1,0:T(8,128)(2,1)S(1)} copy(bf16[8,8,384,128]{3,1,2,0:T(8,128)(2,1)S(1)} %fusion.13) | data formatting | bytes 12582912
  106.7 0.0 copy-start.2
  106.7 3.4 %fusion.17 = f32[3,3,128,128]{3,2,1,0:T(8,128)S(1)} fusion(bf16[64,3,128,128]{3,2,1,0:T(8,128)(2,1)S(1)} %bitcast.55, bf16[64,3,128,128,1]{3,2,1,0,4:T(8,128)(2,1)S(1)} %bitcast.56), kind=kOutput, calls=%fused_computation.17 | convolution fusion | flops 2415919104 | bytes 13172736 | tf_op jit(solution)/shard_map/dot_general | solution.py:30
  110.1 0.2 reshape.78
  110.3 1.3 copy.57
  111.6 6.0 %all-to-all-start.1 = ((f32[64,9,256]{2,1,0:T(8,128)}), f32[64,9,256]{2,1,0:T(8,128)S(1)}, u32[]{:S(2)}, u32[]{:S(2)}) async-start(f32[64,9,256]{2,1,0:T(8,128)} %bitcast.57), calls=%async_computation.1 | async-start | bytes 2097152 | tf_op jit(solution)/shard_map/all_to_all | solution.py:36
  117.7 0.0 copy-done.2
  117.7 0.1 select_reduce_fusion
  117.8 18.9 %all-to-all-done.1 = f32[64,9,256]{2,1,0:T(8,128)S(1)} async-done(((f32[64,9,256]{2,1,0:T(8,128)}), f32[64,9,256]{2,1,0:T(8,128)S(1)}, u32[]{:S(2)}, u32[]{:S(2)}) %all-to-all-start.1) | async-done | bytes 589856 | tf_op jit(solution)/shard_map/all_to_all | solution.py:36
  136.7 1.6 %gather_fusion.1 = f32[64,9,256]{2,1,0:T(8,128)} fusion(f32[64,9,256]{2,1,0:T(8,128)S(1)} %all-to-all-done.1, s32[1024]{0:T(1024)S(1)} %pad_clamp_fusion), kind=kCustom, calls=%fused_computation.1 | custom fusion | bytes 1179904 | tf_op jit(solution)/shard_map/jit(_take)/gather | solution.py:39
  138.3 1.6 %copy.30 = f32[64,9,256]{2,0,1:T(8,128)S(1)} copy(f32[64,9,256]{2,1,0:T(8,128)} %gather_fusion.1) | data formatting | bytes 1179648 | tf_op jit(solution)/shard_map/jit(_take)/gather | solution.py:39
  139.9 0.1 broadcast_select_fusion
  140.1 1.3 collective-permute-start
  141.4 3.0 %collective-permute-start.1 = (f32[1,5,256]{2,0,1:T(1,128)S(1)}, f32[1,5,256]{2,0,1:T(1,128)S(1)}, u32[]{:S(2)}, u32[]{:S(2)}) collective-permute-start(f32[1,5,256]{2,0,1:T(1,128)S(1)} %pad_slice_fusion.1), channel_id=1, source_target_pairs={{0,1},{2,3},{4,5},{6,7},{8,9},{10,11},{12,13},{14,15},{16,17},{18,... | collective-permute-start | bytes 15368 | tf_op jit(solution)/shard_map/ppermute | solution.py:44
  144.5 0.0 collective-permute-done
  144.5 0.7 collective-permute-done.1
  145.2 0.8 fusion.22
  (9 shorter events, 0.1 us)
Async XLA Ops:
  0.0 9.1 %copy-start = (bf16[64,128,128]{2,1,0:T(8,128)(2,1)S(1)}, bf16[64,128,128]{2,1,0:T(8,128)(2,1)}, u32[]{:S(2)}) copy-start(bf16[64,128,128]{2,1,0:T(8,128)(2,1)} %param.6) | copy-start | bytes 6291460
  13.7 86.3 %copy-start.1 = (bf16[64,64]{1,0:T(8,128)(2,1)S(1)}, bf16[64,64]{1,0:T(8,128)(2,1)}, u32[]{:S(2)}) copy-start(bf16[64,64]{1,0:T(8,128)(2,1)} %param.9) | copy-start | bytes 24580
  106.7 11.0 %copy-start.2 = (s32[64]{0:T(128)S(1)}, s32[64]{0:T(128)}, u32[]{:S(2)}) copy-start(s32[64]{0:T(128)} %param.7) | copy-start | bytes 772
  111.6 25.1 %all-to-all-start.1 = ((f32[64,9,256]{2,1,0:T(8,128)}), f32[64,9,256]{2,1,0:T(8,128)S(1)}, u32[]{:S(2)}, u32[]{:S(2)}) async-start(f32[64,9,256]{2,1,0:T(8,128)} %bitcast.57), calls=%async_computation.1 | async-start | bytes 2097152 | tf_op jit(solution)/shard_map/all_to_all | solution.py:36
  140.1 4.4 %collective-permute-start = (f32[1,5,256]{2,0,1:T(1,128)S(1)}, f32[1,5,256]{2,0,1:T(1,128)S(1)}, u32[]{:S(2)}, u32[]{:S(2)}) collective-permute-start(f32[1,5,256]{2,0,1:T(1,128)S(1)} %pad_slice_fusion.2), channel_id=1, source_target_pairs={{1,0},{3,2},{5,4},{7,6},{9,8},{11,10},{13,12},{15,14},{17,16},{19,... | collective-permute-start | bytes 15368 | tf_op jit(solution)/shard_map/ppermute | solution.py:45
  141.4 3.8 %collective-permute-start.1 = (f32[1,5,256]{2,0,1:T(1,128)S(1)}, f32[1,5,256]{2,0,1:T(1,128)S(1)}, u32[]{:S(2)}, u32[]{:S(2)}) collective-permute-start(f32[1,5,256]{2,0,1:T(1,128)S(1)} %pad_slice_fusion.1), channel_id=1, source_target_pairs={{0,1},{2,3},{4,5},{6,7},{8,9},{10,11},{12,13},{14,15},{16,17},{18,... | collective-permute-start | bytes 15368 | tf_op jit(solution)/shard_map/ppermute | solution.py:44

commit v2 on v1

v2 whole, which is shorter than its diff:
```python
import functools

import jax
import jax.numpy as jnp
from jax import lax
from jax.experimental import pallas as pl
from jax.experimental.pallas import tpu as pltpu
from jax.sharding import PartitionSpec as P

MESH = pl.DeviceIdType.MESH
GROUP = 16
CHUNKS = ((0, 32), (32, 32), (64, 32), (96, 16), (112, 16))


def partner(me, step):
    code = lax.rem(step * 27, 64)
    z = lax.rem(me // 16 + code // 16, 4)
    y = lax.rem(me // 4 + code // 4, 4)
    x = lax.rem(me + code, 4)
    return z * 16 + y * 4 + x


def exchange_kernel(
    ints_hbm, orbs_hbm, loc_ref, screen_ref, metric_ref, shares_ref,
    ints, orbs, send, recv, mixer, gram, pieces,
    load_sem, send_sem, recv_sem, out_send_sem, out_recv_sem, own_sem,
):
    me = lax.axis_index("aux")
    core = lax.axis_index("bas")
    n = lax.axis_size("aux")
    tile = orbs.shape[1]
    wide = send.shape[2]
    blocks = ints.shape[0]
    total_blocks = blocks * lax.axis_size("bas")

    load_ints = pltpu.make_async_copy(ints_hbm.at[0], ints, load_sem.at[0])
    load_orbs = pltpu.make_async_copy(orbs_hbm, orbs, load_sem.at[1])
    load_ints.start()
    load_orbs.start()

    barrier = pltpu.get_barrier_semaphore()

    @pl.loop(1, n)
    def _(step):
        pl.semaphore_signal(
            barrier, inc=1, device_id=(partner(me, step), core), device_id_type=MESH
        )

    load_ints.wait()
    load_orbs.wait()

    def half(target):
        block = loc_ref[target]
        rows = ints[block].reshape(wide, tile)
        product = lax.dot_general(
            orbs[target], rows, (((0,), (1,)), ((), ())), preferred_element_type=jnp.float32
        )
        parts = []
        for d in range(3):
            place = core * blocks + block + d - 1
            inside = (place >= 0) & (place < total_blocks)
            keep = jnp.where(inside, screen_ref[0, target, d], 0).astype(jnp.float32)
            parts.append(product[:, d * tile : (d + 1) * tile] * keep)
        return jnp.concatenate(parts, axis=1).astype(jnp.bfloat16)

    def row_copy(step, chunk):
        target = partner(me, step)
        first, count = CHUNKS[chunk]
        return pltpu.make_async_remote_copy(
            src_ref=send.at[target, pl.ds(first, count)],
            dst_ref=recv.at[me, pl.ds(first, count)],
            send_sem=send_sem,
            recv_sem=recv_sem.at[chunk],
            device_id=(target, core),
            device_id_type=MESH,
        )

    pl.semaphore_wait(barrier, n - 1)

    @pl.loop(1, n, unroll=3)
    def _(step):
        target = partner(me, step)
        send[target] = half(target)
        row_copy(step, 0).start()

    for chunk in range(1, len(CHUNKS)):

        @pl.loop(1, n)
        def _(step):
            row_copy(step, chunk).start()

    recv[me] = half(me)

    size = n * GROUP
    gram[...] = jnp.zeros_like(gram)
    spread = (
        lax.broadcasted_iota(jnp.int32, (n, size), 1) // GROUP
        == lax.broadcasted_iota(jnp.int32, (n, size), 0)
    ).astype(jnp.bfloat16)
    step_rows = 128

    @pl.loop(0, size // step_rows)
    def _(part):
        first = part * step_rows
        row = lax.broadcasted_iota(jnp.int32, (step_rows, n), 0) + first
        pick = (row // GROUP == lax.broadcasted_iota(jnp.int32, (step_rows, n), 1))
        rows = jnp.dot(
            pick.astype(jnp.bfloat16), metric_ref[...], preferred_element_type=jnp.float32
        ).astype(jnp.bfloat16)
        full = jnp.dot(rows, spread, preferred_element_type=jnp.float32)
        same = lax.rem(
            lax.broadcasted_iota(jnp.int32, (step_rows, size), 0) + first, GROUP
        ) == lax.rem(lax.broadcasted_iota(jnp.int32, (step_rows, size), 1), GROUP)
        mixer[pl.ds(pl.multiple_of(first, step_rows), step_rows)] = jnp.where(
            same, full, 0.0
        ).astype(jnp.bfloat16)

    for chunk, (first, count) in enumerate(CHUNKS):
        landed = recv.at[pl.ds(0, n - 1), pl.ds(first, count)]
        pltpu.make_async_copy(landed, landed, recv_sem.at[chunk]).wait()
        for start in range(first, first + count, GROUP):
            slab = recv[:, start : start + GROUP, :].reshape(size, wide)
            fitted = jnp.dot(
                mixer[...], slab, preferred_element_type=jnp.float32
            ).astype(jnp.bfloat16)
            gram[...] += lax.dot_general(
                fitted, fitted, (((0,), (0,)), ((), ())), preferred_element_type=jnp.float32
            )

    for d in range(3):
        pieces[:, d] = gram[d * tile : (d + 1) * tile, :].reshape(n, 2, wide)

    def share_copy(step):
        target = partner(me, step)
        return pltpu.make_async_remote_copy(
            src_ref=pieces.at[target],
            dst_ref=shares_ref.at[me],
            send_sem=out_send_sem,
            recv_sem=out_recv_sem,
            device_id=(target, core),
            device_id_type=MESH,
        )

    own = pltpu.make_async_copy(pieces.at[me], shares_ref.at[me], own_sem)
    own.start()

    @pl.loop(1, n)
    def _(step):
        share_copy(step).start()

    own.wait()
    sent = send.at[pl.ds(0, n - 1)]
    pltpu.make_async_copy(sent, sent, send_sem).wait()
    moved = pieces.at[pl.ds(0, n - 1)]
    pltpu.make_async_copy(moved, moved, out_recv_sem).wait()
    pltpu.make_async_copy(moved, moved, out_send_sem).wait()


def body(integrals, orbitals, locality, screen, metric):
    _, block_count, reach, tile, _ = integrals.shape
    n_aux = lax.axis_size("aux")
    wide = reach * tile
    size = n_aux * GROUP
    shares = pl.pallas_call(
        exchange_kernel,
        out_shape=jax.ShapeDtypeStruct((n_aux, reach, 2, wide), jnp.float32),
        in_specs=[
            pl.BlockSpec(memory_space=pl.ANY),
            pl.BlockSpec(memory_space=pl.ANY),
            pl.BlockSpec(memory_space=pltpu.SMEM),
            pl.BlockSpec(memory_space=pltpu.SMEM),
            pl.BlockSpec(memory_space=pltpu.VMEM),
        ],
        out_specs=pl.BlockSpec(memory_space=pl.ANY),
        scratch_shapes=[
            pltpu.VMEM((block_count, reach, tile, tile), jnp.bfloat16),
            pltpu.VMEM((n_aux, tile, tile), jnp.bfloat16),
            pltpu.VMEM((n_aux, tile, wide), jnp.bfloat16),
            pltpu.VMEM((n_aux, tile, wide), jnp.bfloat16),
            pltpu.VMEM((size, size), jnp.bfloat16),
            pltpu.VMEM((wide, wide), jnp.float32),
            pltpu.VMEM((n_aux, reach, 2, wide), jnp.float32),
            pltpu.SemaphoreType.DMA((2,)),
            pltpu.SemaphoreType.DMA,
            pltpu.SemaphoreType.DMA((len(CHUNKS),)),
            pltpu.SemaphoreType.DMA,
            pltpu.SemaphoreType.DMA,
            pltpu.SemaphoreType.DMA,
        ],
        compiler_params=pltpu.CompilerParams(
            collective_id=0, has_side_effects=True, vmem_limit_bytes=48 << 20
        ),
    )(integrals, orbitals, locality, screen, metric)
    ids = jnp.arange(block_count, dtype=jnp.int32)
    order = jnp.sum(jnp.where(locality[None, :] == ids[:, None], ids[None, :], 0), axis=1)
    by_block = jnp.take(shares, order, axis=0).reshape(block_count, reach, 2, reach, tile)
    by_block = jnp.transpose(by_block, (0, 1, 3, 2, 4)).reshape(block_count, reach, reach, -1)
    padded = [
        jnp.pad(by_block[:, d], ((0, 0), (reach - 1 - d, d), (0, 0))) for d in range(reach)
    ]
    from_below = lax.ppermute(padded[2][-1:], "bas", [(0, 1)])
    from_above = lax.ppermute(padded[0][:1], "bas", [(1, 0)])
    lower = jnp.concatenate([padded[0][1:], from_above], axis=0)
    upper = jnp.concatenate([from_below, padded[2][:-1]], axis=0)
    return lower + padded[1] + upper


def solution(mesh):
    placed = (
        P("aux", "bas", None, None, None),
        P("bas", None, None),
        P("bas"),
        P("aux", "bas", None),
        P(),
    )
    return jax.shard_map(
        body, mesh=mesh, in_specs=placed, out_specs=P("bas", None, "aux"), check_vma=False
    )
```

time: 148 us -> 111 us (0.75)
  Pallas kernels: 0 us -> 96.1 us
  blocking collectives: 86.3 us -> 0 us
  waiting for transfers between devices: 19.7 us -> 0.74 us
  matrix products: 12.9 us -> 0 us
  local copies, waits for them, and re-layouts: 13.4 us -> 6.29 us
  starting transfers between devices: 10.4 us -> 4.32 us
    pallas_call x0 -> x1, Pallas kernels: none -> 96.1 us  [body(): pl.pallas_call(exchange_kernel, out_shape=jax.ShapeDtypeStruct((n_aux, re...]
    all_to_all x1 -> x0, blocking collectives: 86.3 us -> none  [body(): lax.all_to_all(half_rows, 'aux', split_axis=0, concat_axis=1, tiled=True)]
    all_to_all x1 -> x0, waiting for transfers between devices: 18.9 us -> none  [body(): lax.all_to_all(pieces, 'aux', split_axis=0, concat_axis=0, tiled=True)]
    dot_general x3 -> x0, matrix products: 12.9 us -> none  [the longest x1 4.89 us: metric_apply(): jnp.dot(metric, slab_rows.reshape(slab_rows.shape[0], -1), preferred_elem...]
    gather x3, local copies, waits for them, and re-layouts: 9.96 us -> 1.53 us  [body(): jnp.take(shares, order, axis=0).reshape(block_count, reach, 2, reach, tile)]
    all_to_all x1 -> x0, starting transfers between devices: 6.04 us -> none  [body(): lax.all_to_all(pieces, 'aux', split_axis=0, concat_axis=0, tiled=True)]
    unnamed x7, local copies, waits for them, and re-layouts: 1.76 us -> 3.73 us
  transfers between devices with their start and end apart: 3 -> 2, of which waited for: 2 -> 1; matrix products, arithmetic and copies ran while one was open for 0% -> 0% of each run, Pallas kernels for 0% -> 0%
where the time goes in v2:
time: 111 us; the launch traced here: 109 us
  Pallas kernels  96.1 us (87%)
  local copies, waits for them, and re-layouts  6.29 us (6%)
  starting transfers between devices  4.32 us (4%)
  other arithmetic  1.8 us (2%)
    pallas_call x1, Pallas kernels, body(): pl.pallas_call(exchange_kernel, out_shape=jax.ShapeDtypeStruct((n_aux, re...  96.1 us
    unnamed x7, local copies, waits for them, and re-layouts  3.73 us
    ppermute x1, starting transfers between devices, body(): from_below = lax.ppermute(padded[2][-1:], 'bas', [(0, 1)])  3.03 us
  transfers between devices with their start and end apart: 2, of which 1 were waited for; matrix products, arithmetic and copies ran while one was open for 0% of the time, Pallas kernels for 0%

profile of v2, /device:TPU:0, one launch (start us, length us, event | category | flops | bytes accessed | tf_op | source)
XLA Modules:
  0.0 109.4 jit_solution(5276269470168217092)
XLA Ops:
  0.0 0.8 select_reduce_fusion
  0.8 0.8 copy.13.screen_ref
  1.6 0.0 copy-start
  1.6 1.6 %copy-done = bf16[64,128,128]{2,1,0:T(8,128)(2,1)S(1)} copy-done((bf16[64,128,128]{2,1,0:T(8,128)(2,1)S(1)}, bf16[64,128,128]{2,1,0:T(8,128)(2,1)}, u32[]{:S(2)}) %copy-start) | copy-done | bytes 2097176
  3.2 0.0 copy-start.1
  3.2 0.7 copy-done.1
  3.9 0.0 copy-start.2
  3.9 0.7 copy-done.2
  4.5 96.1 %shard_map.55 = f32[64,3,2,384]{3,2,1,0:T(2,128)S(1)} custom-call(bf16[1,64,3,128,128]{4,3,2,1,0:T(8,128)(2,1)} %ints_hbm.1, bf16[64,128,128]{2,1,0:T(8,128)(2,1)S(1)} %copy-done, s32[64]{0:T(128)S(1)} %copy-done.2, s32[1,64,3]{2,1,0:T(8,128)S(1)} %copy.13.screen_ref, bf16[64,64]{1,0:T(8,128)(2,1)S(1)} %copy-done.1), custom_call_target="tpu_custom_call" | custom-call | tf_op jit(solution)/shard_map/pallas_call | solution.py:164
  100.6 1.3 %gather_fusion = f32[64,3,2,384]{3,2,1,0:T(2,128)S(1)} fusion(f32[64,3,2,384]{3,2,1,0:T(2,128)S(1)} %shard_map.55, s32[1024]{0:T(1024)S(1)} %pad_clamp_fusion), kind=kCustom, calls=%fused_computation | custom fusion | bytes 1179904 | tf_op jit(solution)/shard_map/jit(_take)/gather | solution.py:196
  101.9 0.2 gather.7
  102.2 0.2 select_bitcast_fusion
  102.4 0.5 copy.15
  102.9 0.5 reshape.24
  103.4 1.3 %collective-permute-start = (f32[1,5,256]{2,0,1:T(1,128)S(1)}, f32[1,5,256]{2,0,1:T(1,128)S(1)}, u32[]{:S(2)}, u32[]{:S(2)}) collective-permute-start(f32[1,5,256]{2,0,1:T(1,128)S(1)} %pad_slice_fusion.2), channel_id=1, source_target_pairs={{1,0},{3,2},{5,4},{7,6},{9,8},{11,10},{13,12},{15,14},{17,16},{19,... | collective-permute-start | bytes 15368 | tf_op jit(solution)/shard_map/ppermute | solution.py:202
  104.7 3.0 %collective-permute-start.1 = (f32[1,5,256]{2,0,1:T(1,128)S(1)}, f32[1,5,256]{2,0,1:T(1,128)S(1)}, u32[]{:S(2)}, u32[]{:S(2)}) collective-permute-start(f32[1,5,256]{2,0,1:T(1,128)S(1)} %pad_slice_fusion.1), channel_id=1, source_target_pairs={{0,1},{2,3},{4,5},{6,7},{8,9},{10,11},{12,13},{14,15},{16,17},{18,... | collective-permute-start | bytes 15368 | tf_op jit(solution)/shard_map/ppermute | solution.py:201
  107.8 0.0 collective-permute-done
  107.8 0.7 collective-permute-done.1
  108.6 0.8 fusion
  (8 shorter events, 0.2 us)
Async XLA Ops:
  1.6 1.6 %copy-start = (bf16[64,128,128]{2,1,0:T(8,128)(2,1)S(1)}, bf16[64,128,128]{2,1,0:T(8,128)(2,1)}, u32[]{:S(2)}) copy-start(bf16[64,128,128]{2,1,0:T(8,128)(2,1)} %orbs_hbm.1) | copy-start | bytes 6291460
  3.2 0.7 copy-start.1
  3.9 0.7 copy-start.2
  103.4 4.4 %collective-permute-start = (f32[1,5,256]{2,0,1:T(1,128)S(1)}, f32[1,5,256]{2,0,1:T(1,128)S(1)}, u32[]{:S(2)}, u32[]{:S(2)}) collective-permute-start(f32[1,5,256]{2,0,1:T(1,128)S(1)} %pad_slice_fusion.2), channel_id=1, source_target_pairs={{1,0},{3,2},{5,4},{7,6},{9,8},{11,10},{13,12},{15,14},{17,16},{19,... | collective-permute-start | bytes 15368 | tf_op jit(solution)/shard_map/ppermute | solution.py:202
  104.7 3.8 %collective-permute-start.1 = (f32[1,5,256]{2,0,1:T(1,128)S(1)}, f32[1,5,256]{2,0,1:T(1,128)S(1)}, u32[]{:S(2)}, u32[]{:S(2)}) collective-permute-start(f32[1,5,256]{2,0,1:T(1,128)S(1)} %pad_slice_fusion.1), channel_id=1, source_target_pairs={{0,1},{2,3},{4,5},{6,7},{8,9},{10,11},{12,13},{14,15},{16,17},{18,... | collective-permute-start | bytes 15368 | tf_op jit(solution)/shard_map/ppermute | solution.py:201

commit v3 on v2

--- a/solution.py
+++ b/solution.py
@@ -21,9 +21,10 @@
 
 
 def exchange_kernel(
-    ints_hbm, orbs_hbm, loc_ref, screen_ref, metric_ref, shares_ref,
-    ints, orbs, send, recv, mixer, gram, pieces,
-    load_sem, send_sem, recv_sem, out_send_sem, out_recv_sem, own_sem,
+    ints_hbm, orbs_hbm, loc_hbm, screen_hbm, metric_hbm, band_ref,
+    ints, orbs, loc_ref, screen_ref, order_ref, metric_ref, send, recv, mixer, gram, pieces,
+    shares, rim, near, rows,
+    load_sem, send_sem, recv_sem, out_send_sem, out_recv_sem, own_sem, rim_sem,
 ):
     me = lax.axis_index("aux")
     core = lax.axis_index("bas")
@@ -33,12 +34,23 @@
     blocks = ints.shape[0]
     total_blocks = blocks * lax.axis_size("bas")
 
-    load_ints = pltpu.make_async_copy(ints_hbm.at[0], ints, load_sem.at[0])
-    load_orbs = pltpu.make_async_copy(orbs_hbm, orbs, load_sem.at[1])
-    load_ints.start()
-    load_orbs.start()
+    loads = [
+        pltpu.make_async_copy(source, target, load_sem.at[place])
+        for place, (source, target) in enumerate(
+            (
+                (ints_hbm.at[0], ints),
+                (orbs_hbm, orbs),
+                (loc_hbm, loc_ref),
+                (screen_hbm, screen_ref),
+                (metric_hbm, metric_ref),
+            )
+        )
+    ]
+    for load in loads:
+        load.start()
 
     barrier = pltpu.get_barrier_semaphore()
+    pl.semaphore_signal(barrier, inc=1, device_id=(me, 1 - core), device_id_type=MESH)
 
     @pl.loop(1, n)
     def _(step):
@@ -46,8 +58,8 @@
             barrier, inc=1, device_id=(partner(me, step), core), device_id_type=MESH
         )
 
-    load_ints.wait()
-    load_orbs.wait()
+    for load in loads:
+        load.wait()
 
     def half(target):
         block = loc_ref[target]
@@ -59,7 +71,7 @@
         for d in range(3):
             place = core * blocks + block + d - 1
             inside = (place >= 0) & (place < total_blocks)
-            keep = jnp.where(inside, screen_ref[0, target, d], 0).astype(jnp.float32)
+            keep = jnp.where(inside, screen_ref[d, 0, target], 0).astype(jnp.float32)
             parts.append(product[:, d * tile : (d + 1) * tile] * keep)
         return jnp.concatenate(parts, axis=1).astype(jnp.bfloat16)
 
@@ -75,7 +87,7 @@
             device_id_type=MESH,
         )
 
-    pl.semaphore_wait(barrier, n - 1)
+    pl.semaphore_wait(barrier, n)
 
     @pl.loop(1, n, unroll=3)
     def _(step):
@@ -90,6 +102,13 @@
             row_copy(step, chunk).start()
 
     recv[me] = half(me)
+
+    @pl.loop(0, blocks)
+    def _(block):
+        def find(target, found):
+            return jnp.where(loc_ref[target] == block, target, found)
+
+        order_ref[block] = lax.fori_loop(0, blocks, find, jnp.int32(0), unroll=8)
 
     size = n * GROUP
     gram[...] = jnp.zeros_like(gram)
@@ -134,26 +153,67 @@
         target = partner(me, step)
         return pltpu.make_async_remote_copy(
             src_ref=pieces.at[target],
-            dst_ref=shares_ref.at[me],
+            dst_ref=shares.at[me],
             send_sem=out_send_sem,
             recv_sem=out_recv_sem,
             device_id=(target, core),
             device_id_type=MESH,
         )
 
-    own = pltpu.make_async_copy(pieces.at[me], shares_ref.at[me], own_sem)
-    own.start()
-
     @pl.loop(1, n)
     def _(step):
         share_copy(step).start()
 
-    own.wait()
+    own = pltpu.make_async_copy(pieces.at[me], shares.at[me], own_sem)
+    own.start()
     sent = send.at[pl.ds(0, n - 1)]
     pltpu.make_async_copy(sent, sent, send_sem).wait()
+    own.wait()
     moved = pieces.at[pl.ds(0, n - 1)]
     pltpu.make_async_copy(moved, moved, out_recv_sem).wait()
+    edge = jnp.where(core == 0, blocks - 1, 0)
+    rim[...] = shares[order_ref[edge], 2 * (1 - core)]
+    rim_copy = pltpu.make_async_remote_copy(
+        src_ref=rim,
+        dst_ref=near,
+        send_sem=rim_sem.at[0],
+        recv_sem=rim_sem.at[1],
+        device_id=(me, 1 - core),
+        device_id_type=MESH,
+    )
+    rim_copy.start()
+
+    def put(place, pieces_of_d):
+        for e in range(5):
+            terms = [
+                piece[:, (e - 2 + d) * tile : (e - 1 + d) * tile]
+                for d, piece in enumerate(pieces_of_d)
+                if 0 <= e - 2 + d < 3
+            ]
+            rows[e, place] = functools.reduce(lambda left, right: left + right, terms)
+
+    @pl.loop(1, blocks - 1, unroll=2)
+    def _(place):
+        put(place, [shares[order_ref[place + 1 - d], d] for d in range(3)])
+
+    def lay(first, count):
+        for e in range(5):
+            for b in range(2):
+                band_ref[e, first : first + count, b * tile : (b + 1) * tile] = rows[
+                    e, first : first + count, b
+                ]
+
+    lay(8, blocks - 16)
     pltpu.make_async_copy(moved, moved, out_send_sem).wait()
+    rim_copy.wait()
+    other = near[...]
+    none = jnp.zeros_like(other)
+    first_rows = [shares[order_ref[1 - d], d] for d in range(2)]
+    put(0, first_rows + [jnp.where(core == 0, none, other)])
+    last_rows = [shares[order_ref[blocks - d], d] for d in range(1, 3)]
+    put(blocks - 1, [jnp.where(core == 0, other, none)] + last_rows)
+    lay(0, 8)
+    lay(blocks - 8, 8)
 
 
 def body(integrals, orbitals, locality, screen, metric):
@@ -161,48 +221,41 @@
     n_aux = lax.axis_size("aux")
     wide = reach * tile
     size = n_aux * GROUP
-    shares = pl.pallas_call(
+    hbm = pl.BlockSpec(memory_space=pltpu.HBM)
+    band = pl.pallas_call(
         exchange_kernel,
-        out_shape=jax.ShapeDtypeStruct((n_aux, reach, 2, wide), jnp.float32),
-        in_specs=[
-            pl.BlockSpec(memory_space=pl.ANY),
-            pl.BlockSpec(memory_space=pl.ANY),
-            pl.BlockSpec(memory_space=pltpu.SMEM),
-            pl.BlockSpec(memory_space=pltpu.SMEM),
-            pl.BlockSpec(memory_space=pltpu.VMEM),
-        ],
-        out_specs=pl.BlockSpec(memory_space=pl.ANY),
+        out_shape=jax.ShapeDtypeStruct((2 * reach - 1, block_count, 2 * tile), jnp.float32),
+        in_specs=[hbm] * 5,
+        out_specs=pl.BlockSpec(memory_space=pltpu.VMEM),
         scratch_shapes=[
             pltpu.VMEM((block_count, reach, tile, tile), jnp.bfloat16),
             pltpu.VMEM((n_aux, tile, tile), jnp.bfloat16),
+            pltpu.SMEM((block_count,), jnp.int32),
+            pltpu.SMEM((reach, 1, n_aux), jnp.int32),
+            pltpu.SMEM((block_count,), jnp.int32),
+            pltpu.VMEM((n_aux, n_aux), jnp.bfloat16),
             pltpu.VMEM((n_aux, tile, wide), jnp.bfloat16),
             pltpu.VMEM((n_aux, tile, wide), jnp.bfloat16),
             pltpu.VMEM((size, size), jnp.bfloat16),
             pltpu.VMEM((wide, wide), jnp.float32),
             pltpu.VMEM((n_aux, reach, 2, wide), jnp.float32),
+            pltpu.VMEM((n_aux, reach, 2, wide), jnp.float32),
+            pltpu.VMEM((2, wide), jnp.float32),
+            pltpu.VMEM((2, wide), jnp.float32),
+            pltpu.VMEM((2 * reach - 1, block_count, 2, tile), jnp.float32),
+            pltpu.SemaphoreType.DMA((5,)),
+            pltpu.SemaphoreType.DMA,
+            pltpu.SemaphoreType.DMA((len(CHUNKS),)),
+            pltpu.SemaphoreType.DMA,
+            pltpu.SemaphoreType.DMA,
+            pltpu.SemaphoreType.DMA,
             pltpu.SemaphoreType.DMA((2,)),
-            pltpu.SemaphoreType.DMA,
-            pltpu.SemaphoreType.DMA((len(CHUNKS),)),
-            pltpu.SemaphoreType.DMA,
-            pltpu.SemaphoreType.DMA,
-            pltpu.SemaphoreType.DMA,
         ],
         compiler_params=pltpu.CompilerParams(
-            collective_id=0, has_side_effects=True, vmem_limit_bytes=48 << 20
+            collective_id=0, has_side_effects=True, vmem_limit_bytes=63 << 20
         ),
-    )(integrals, orbitals, locality, screen, metric)
-    ids = jnp.arange(block_count, dtype=jnp.int32)
-    order = jnp.sum(jnp.where(locality[None, :] == ids[:, None], ids[None, :], 0), axis=1)
-    by_block = jnp.take(shares, order, axis=0).reshape(block_count, reach, 2, reach, tile)
-    by_block = jnp.transpose(by_block, (0, 1, 3, 2, 4)).reshape(block_count, reach, reach, -1)
-    padded = [
-        jnp.pad(by_block[:, d], ((0, 0), (reach - 1 - d, d), (0, 0))) for d in range(reach)
-    ]
-    from_below = lax.ppermute(padded[2][-1:], "bas", [(0, 1)])
-    from_above = lax.ppermute(padded[0][:1], "bas", [(1, 0)])
-    lower = jnp.concatenate([padded[0][1:], from_above], axis=0)
-    upper = jnp.concatenate([from_below, padded[2][:-1]], axis=0)
-    return lower + padded[1] + upper
+    )(integrals, orbitals, locality, jnp.transpose(screen, (2, 0, 1)), metric)
+    return jnp.transpose(band, (1, 0, 2))
 
 
 def solution(mesh):

time: 111 us -> 99.5 us (0.90)
  local copies, waits for them, and re-layouts: 6.29 us -> 1.72 us
  starting transfers between devices: 4.32 us -> 0 us
  other arithmetic: 1.8 us -> 0 us
    ppermute x2 -> x0, starting transfers between devices: 4.32 us -> none  [the longest x1 3.03 us: body(): from_below = lax.ppermute(padded[2][-1:], 'bas', [(0, 1)])]
    unnamed x7 -> x1, local copies, waits for them, and re-layouts: 3.73 us -> 1.72 us
    gather x3 -> x0, local copies, waits for them, and re-layouts: 1.53 us -> none  [body(): jnp.take(shares, order, axis=0).reshape(block_count, reach, 2, reach, tile)]
  transfers between devices with their start and end apart: 2 -> 0, of which waited for: 1 -> 0; matrix products, arithmetic and copies ran while one was open for 0% -> 0% of each run, Pallas kernels for 0% -> 0%
where the time goes in v3:
time: 99.5 us; the launch traced here: 98.1 us
  Pallas kernels  96.4 us (97%)
  local copies, waits for them, and re-layouts  1.72 us (2%)
    pallas_call x1, Pallas kernels, body(): pl.pallas_call(exchange_kernel, out_shape=jax.ShapeDtypeStruct((2 * reach...  96.4 us

profile of v3, /device:TPU:0, one launch (start us, length us, event | category | flops | bytes accessed | tf_op | source)
XLA Modules:
  0.0 98.1 jit_solution(15245895967839451140)
XLA Ops:
  0.0 96.4 %shard_map.55 = f32[5,64,256]{2,1,0:T(8,128)} custom-call(bf16[1,64,3,128,128]{4,3,2,1,0:T(8,128)(2,1)} %ints_hbm.1, bf16[64,128,128]{2,1,0:T(8,128)(2,1)} %orbs_hbm.1, s32[64]{0:T(128)} %loc_hbm.1, s32[3,1,64]{2,1,0:T(1,128)} %bitcast.3, bf16[64,64]{1,0:T(8,128)(2,1)} %metric_hbm.1), custom_call_target="tpu_custom_call" | custom-call | tf_op jit(solution)/shard_map/pallas_call | solution.py:225
  96.4 1.7 %copy.7 = f32[64,5,256]{2,0,1:T(8,128)} copy(f32[64,5,256]{2,0,1:T(8,128)} %bitcast.2) | data formatting | bytes 655360

commit v4 on v3

--- a/solution.py
+++ b/solution.py
@@ -22,8 +22,7 @@
 
 def exchange_kernel(
     ints_hbm, orbs_hbm, loc_hbm, screen_hbm, metric_hbm, band_ref,
-    ints, orbs, loc_ref, screen_ref, order_ref, metric_ref, send, recv, mixer, gram, pieces,
-    shares, rim, near, rows,
+    ints, orbs, loc_ref, screen_ref, order_ref, metric_ref, send, recv, mixer, gram, shares,
     load_sem, send_sem, recv_sem, out_send_sem, out_recv_sem, own_sem, rim_sem,
 ):
     me = lax.axis_index("aux")
@@ -33,14 +32,16 @@
     wide = send.shape[2]
     blocks = ints.shape[0]
     total_blocks = blocks * lax.axis_size("bas")
+    edge = jnp.where(core == 0, blocks - 1, 0)
+    other_edge = jnp.where(core == 0, 0, blocks - 1)
 
     loads = [
         pltpu.make_async_copy(source, target, load_sem.at[place])
         for place, (source, target) in enumerate(
             (
+                (loc_hbm, loc_ref),
                 (ints_hbm.at[0], ints),
                 (orbs_hbm, orbs),
-                (loc_hbm, loc_ref),
                 (screen_hbm, screen_ref),
                 (metric_hbm, metric_ref),
             )
@@ -50,7 +51,6 @@
         load.start()
 
     barrier = pltpu.get_barrier_semaphore()
-    pl.semaphore_signal(barrier, inc=1, device_id=(me, 1 - core), device_id_type=MESH)
 
     @pl.loop(1, n)
     def _(step):
@@ -58,20 +58,32 @@
             barrier, inc=1, device_id=(partner(me, step), core), device_id_type=MESH
         )
 
-    for load in loads:
+    pl.semaphore_signal(
+        barrier, inc=1, device_id=(other_edge, 1 - core), device_id_type=MESH
+    )
+    loads[0].wait()
+
+    @pl.loop(0, blocks)
+    def _(block):
+        found = jnp.int32(0)
+        for index in range(blocks):
+            found = jnp.where(loc_ref[index] == block, index, found)
+        order_ref[block] = found
+
+    for load in loads[1:]:
         load.wait()
 
-    def half(target):
-        block = loc_ref[target]
+    def half(block):
+        index = order_ref[block]
         rows = ints[block].reshape(wide, tile)
         product = lax.dot_general(
-            orbs[target], rows, (((0,), (1,)), ((), ())), preferred_element_type=jnp.float32
+            orbs[index], rows, (((0,), (1,)), ((), ())), preferred_element_type=jnp.float32
         )
         parts = []
         for d in range(3):
             place = core * blocks + block + d - 1
             inside = (place >= 0) & (place < total_blocks)
-            keep = jnp.where(inside, screen_ref[d, 0, target], 0).astype(jnp.float32)
+            keep = jnp.where(inside, screen_ref[d, 0, index], 0).astype(jnp.float32)
             parts.append(product[:, d * tile : (d + 1) * tile] * keep)
         return jnp.concatenate(parts, axis=1).astype(jnp.bfloat16)
 
@@ -87,7 +99,7 @@
             device_id_type=MESH,
         )
 
-    pl.semaphore_wait(barrier, n)
+    pl.semaphore_wait(barrier, jnp.where(me == edge, 2 * n - 1, n - 1))
 
     @pl.loop(1, n, unroll=3)
     def _(step):
@@ -102,13 +114,6 @@
             row_copy(step, chunk).start()
 
     recv[me] = half(me)
-
-    @pl.loop(0, blocks)
-    def _(block):
-        def find(target, found):
-            return jnp.where(loc_ref[target] == block, target, found)
-
-        order_ref[block] = lax.fori_loop(0, blocks, find, jnp.int32(0), unroll=8)
 
     size = n * GROUP
     gram[...] = jnp.zeros_like(gram)
@@ -142,78 +147,80 @@
             fitted = jnp.dot(
                 mixer[...], slab, preferred_element_type=jnp.float32
             ).astype(jnp.bfloat16)
-            gram[...] += lax.dot_general(
+            product = lax.dot_general(
                 fitted, fitted, (((0,), (0,)), ((), ())), preferred_element_type=jnp.float32
             )
-
-    for d in range(3):
-        pieces[:, d] = gram[d * tile : (d + 1) * tile, :].reshape(n, 2, wide)
+            for d in range(3):
+                for d2 in range(3):
+                    gram[3 * d + d2] += product[
+                        d * tile : (d + 1) * tile, d2 * tile : (d2 + 1) * tile
+                    ]
+
+    pieces = gram.reshape(9, n, 2, tile)
+    top = blocks + 8
 
     def share_copy(step):
         target = partner(me, step)
         return pltpu.make_async_remote_copy(
-            src_ref=pieces.at[target],
-            dst_ref=shares.at[me],
+            src_ref=pieces.at[:, target],
+            dst_ref=shares.at[:, :, me + 8, 0],
             send_sem=out_send_sem,
             recv_sem=out_recv_sem,
             device_id=(target, core),
             device_id_type=MESH,
         )
 
+    def rim_copy(target):
+        return pltpu.make_async_remote_copy(
+            src_ref=pieces.at[pl.ds(6 * (1 - core), 3), target],
+            dst_ref=shares.at[pl.ds(6 * (1 - core), 3), :, jnp.where(core == 0, 7, top), 0],
+            send_sem=rim_sem.at[0],
+            recv_sem=rim_sem.at[1],
+            device_id=(target, 1 - core),
+            device_id_type=MESH,
+        )
+
+    @pl.when(me == edge)
+    def _():
+        @pl.loop(0, n)
+        def _(target):
+            rim_copy(target).start()
+
     @pl.loop(1, n)
     def _(step):
         share_copy(step).start()
 
-    own = pltpu.make_async_copy(pieces.at[me], shares.at[me], own_sem)
+    own = pltpu.make_async_copy(pieces.at[:, me], shares.at[:, :, me + 8, 0], own_sem)
     own.start()
+    shares[pl.ds(6 * (1 - core), 3), :, jnp.where(core == 0, 7, top)] = jnp.zeros(
+        (3, 2, 1, tile), jnp.float32
+    )
     sent = send.at[pl.ds(0, n - 1)]
     pltpu.make_async_copy(sent, sent, send_sem).wait()
     own.wait()
-    moved = pieces.at[pl.ds(0, n - 1)]
+    moved = pieces.at[:, pl.ds(0, n - 1)]
     pltpu.make_async_copy(moved, moved, out_recv_sem).wait()
-    edge = jnp.where(core == 0, blocks - 1, 0)
-    rim[...] = shares[order_ref[edge], 2 * (1 - core)]
-    rim_copy = pltpu.make_async_remote_copy(
-        src_ref=rim,
-        dst_ref=near,
-        send_sem=rim_sem.at[0],
-        recv_sem=rim_sem.at[1],
-        device_id=(me, 1 - core),
-        device_id_type=MESH,
-    )
-    rim_copy.start()
-
-    def put(place, pieces_of_d):
-        for e in range(5):
+    one = pieces.at[pl.ds(0, 3), 0]
+    pltpu.make_async_copy(one, one, rim_sem.at[1]).wait()
+
+    flat = shares.reshape(9, 2, blocks + 16, tile)
+    for e in range(5):
+        for b in range(2):
             terms = [
-                piece[:, (e - 2 + d) * tile : (e - 1 + d) * tile]
-                for d, piece in enumerate(pieces_of_d)
+                flat[3 * d + e - 2 + d, b, 9 - d : 9 - d + blocks, :]
+                for d in range(3)
                 if 0 <= e - 2 + d < 3
             ]
-            rows[e, place] = functools.reduce(lambda left, right: left + right, terms)
-
-    @pl.loop(1, blocks - 1, unroll=2)
-    def _(place):
-        put(place, [shares[order_ref[place + 1 - d], d] for d in range(3)])
-
-    def lay(first, count):
-        for e in range(5):
-            for b in range(2):
-                band_ref[e, first : first + count, b * tile : (b + 1) * tile] = rows[
-                    e, first : first + count, b
-                ]
-
-    lay(8, blocks - 16)
+            band_ref[e, :, b * tile : (b + 1) * tile] = functools.reduce(
+                lambda left, right: left + right, terms
+            )
+
     pltpu.make_async_copy(moved, moved, out_send_sem).wait()
-    rim_copy.wait()
-    other = near[...]
-    none = jnp.zeros_like(other)
-    first_rows = [shares[order_ref[1 - d], d] for d in range(2)]
-    put(0, first_rows + [jnp.where(core == 0, none, other)])
-    last_rows = [shares[order_ref[blocks - d], d] for d in range(1, 3)]
-    put(blocks - 1, [jnp.where(core == 0, other, none)] + last_rows)
-    lay(0, 8)
-    lay(blocks - 8, 8)
+
+    @pl.when(me == edge)
+    def _():
+        every = pieces.at[pl.ds(0, 3)]
+        pltpu.make_async_copy(every, every, rim_sem.at[0]).wait()
 
 
 def body(integrals, orbitals, locality, screen, metric):
@@ -237,12 +244,8 @@
             pltpu.VMEM((n_aux, tile, wide), jnp.bfloat16),
             pltpu.VMEM((n_aux, tile, wide), jnp.bfloat16),
             pltpu.VMEM((size, size), jnp.bfloat16),
-            pltpu.VMEM((wide, wide), jnp.float32),
-            pltpu.VMEM((n_aux, reach, 2, wide), jnp.float32),
-            pltpu.VMEM((n_aux, reach, 2, wide), jnp.float32),
-            pltpu.VMEM((2, wide), jnp.float32),
-            pltpu.VMEM((2, wide), jnp.float32),
-            pltpu.VMEM((2 * reach - 1, block_count, 2, tile), jnp.float32),
+            pltpu.VMEM((reach * reach, tile, tile), jnp.float32),
+            pltpu.VMEM((reach * reach, 2, block_count + 16, 1, tile), jnp.float32),
             pltpu.SemaphoreType.DMA((5,)),
             pltpu.SemaphoreType.DMA,
             pltpu.SemaphoreType.DMA((len(CHUNKS),)),

time: 99.5 us -> 98.6 us (level)
  no operation moved by 1% of the time
where the time goes in v4:
time: 98.6 us; the launch traced here: 98 us
  Pallas kernels  96.3 us (98%)
  local copies, waits for them, and re-layouts  1.72 us (2%)
    pallas_call x1, Pallas kernels, body(): pl.pallas_call(exchange_kernel, out_shape=jax.ShapeDtypeStruct((2 * reach...  96.3 us

profile of v4, /device:TPU:0, one launch (start us, length us, event | category | flops | bytes accessed | tf_op | source)
XLA Modules:
  0.0 98.0 jit_solution(15942580752681718211)
XLA Ops:
  0.0 96.3 %shard_map.55 = f32[5,64,256]{2,1,0:T(8,128)} custom-call(bf16[1,64,3,128,128]{4,3,2,1,0:T(8,128)(2,1)} %ints_hbm.1, bf16[64,128,128]{2,1,0:T(8,128)(2,1)} %orbs_hbm.1, s32[64]{0:T(128)} %loc_hbm.1, s32[3,1,64]{2,1,0:T(1,128)} %bitcast.3, bf16[64,64]{1,0:T(8,128)(2,1)} %metric_hbm.1), custom_call_target="tpu_custom_call" | custom-call | tf_op jit(solution)/shard_map/pallas_call | solution.py:232
  96.3 1.7 %copy.7 = f32[64,5,256]{2,0,1:T(8,128)} copy(f32[64,5,256]{2,0,1:T(8,128)} %bitcast.2) | data formatting | bytes 655360
